TPU v7x, 32 devices: a whole 2x2x4 slice. The times are simulated.
32 devices in a mesh: group: 2 (over y), seq: 4 (over z), head: 4 (over x, core).
Axes of the slice: x: 2, y: 2, z: 4, core: 2. Of those that a mesh axis runs over, the one named last changes fastest.
Arguments:
- q_lin: bfloat16 [3072, 2048], P(('group', 'seq'), 'head'), parts along dimension 0, may hold values from -6 to 6
- k_lin: bfloat16 [3072, 2048], P(('group', 'seq'), 'head'), parts along dimension 0, may hold values from -6 to 6
- v_lin: bfloat16 [3072, 2048], P(('group', 'seq'), 'head'), parts along dimension 0, may hold values from -6 to 6
- q_soft: bfloat16 [3072, 2048], P(('group', 'seq'), 'head'), parts along dimension 0, may hold values from -5 to 5
- k_soft: bfloat16 [3072, 2048], P(('group', 'seq'), 'head'), parts along dimension 0, may hold values from -5 to 5
- v_soft: bfloat16 [3072, 2048], P(('group', 'seq'), 'head'), parts along dimension 0, may hold values from -6 to 6
- segment: int32 [3072], P(('group', 'seq')), parts along dimension 0, may hold values from 0 to 3, as said below
Outputs:
- mixed_lin: bfloat16 [3072, 2048], P(('group', 'seq'), 'head'), parts along dimension 0
- mixed_soft: bfloat16 [3072, 2048], P(('group', 'seq'), 'head'), parts along dimension 0
There are 2 independent parts, one for each index of `group`. A program takes and returns all parts, laid end to end along the dimension named above; each array names one. Nothing has to cross between parts.
Inputs may be any that keep to these rules, and one draw needn't show every extreme that they name: `segment`: document numbers never fall along the list; each of the 4 documents has 1 to 960 tokens and one has exactly 960.
All inputs are finite; a program needn't handle non-finite values.
Results may differ from a plain program's by a relative error of at most 0.0075.
Values may be sent and summed in bfloat16 or wider, within the bound.
A program may use at most 128 MiB of HBM per device.

v0:
```python
import jax
import jax.numpy as jnp
from jax import lax
from jax.sharding import PartitionSpec as P

HEAD_DIM = 128


def entering(shard, axis, combine, identity):
    devices, position = (lax.axis_size(axis), lax.axis_index(axis))
    everything = jax.tree.map(
        lambda part, kind: lax.all_gather(part.astype(kind), axis),
        shard,
        (jnp.bfloat16, jnp.bfloat16),
    )
    start = jax.tree.map(
        lambda part, zero: jnp.broadcast_to(jnp.asarray(zero, part.dtype), part.shape),
        shard,
        identity,
    )

    def hop(k, before):
        reached = k < position
        new = combine(
            before, jax.tree.map(lambda part, own: part[k].astype(own.dtype), everything, shard)
        )
        return jax.tree.map(lambda a, b: jnp.where(reached, a, b), new, before)

    return lax.fori_loop(0, devices, hop, start)


def shifted(value, axis, steps):
    count = lax.axis_size(axis)
    initial, last = (max(0, -steps), min(count, count - steps))
    return lax.ppermute(value, axis, [(source, source + steps) for source in range(initial, last)])


def join_states(earlier, later):
    early_state, early_last = earlier
    late_state, late_last = later
    joined = late_state + jnp.where(early_last == late_last, early_state, 0.0)
    memory_state = jnp.where(late_last < 0.0, early_state, joined)
    last_id = jnp.where(late_last < 0.0, early_last, late_last)
    return (memory_state, last_id)


def on_device(q_lin, k_lin, v_lin, q_soft, k_soft, v_soft, segment):
    rows = q_lin.shape[0]
    heads_here = q_lin.shape[1] // HEAD_DIM
    shape = (rows, heads_here, HEAD_DIM)
    single_query = q_lin.reshape(shape)
    single_key = k_lin.reshape(shape)
    single_value = v_lin.reshape(shape)
    places = jnp.arange(rows, dtype=jnp.int32)
    me_index = lax.axis_index("seq")
    scores = jnp.einsum(
        "thd,shd->hts", single_query, single_key, preferred_element_type=jnp.float32
    )
    same = (segment[:, None] == segment[None, :]) & (places[:, None] >= places[None, :])
    scores = jnp.where(same[None], scores, 0.0)
    inner = jnp.einsum(
        "hts,shd->thd", scores, single_value.astype(jnp.float32), precision=lax.Precision.HIGHEST
    )
    retain_mask = (segment == segment[-1]).astype(single_key.dtype)
    local_state = jnp.einsum(
        "piy,piw->iyw",
        single_key * retain_mask[:, None, None],
        single_value,
        preferred_element_type=jnp.float32,
    )
    own_last = segment[-1].astype(jnp.float32)
    empty = jnp.zeros((heads_here, HEAD_DIM, HEAD_DIM), jnp.float32)
    arriving_state, carried = entering(
        (local_state, own_last), "seq", join_states, (empty, jnp.float32(-1.0))
    )
    apply = (segment.astype(jnp.float32) == carried).astype(jnp.float32)
    outer_product = jnp.einsum(
        "upi,pis->ups",
        single_query.astype(jnp.float32),
        arriving_state,
        precision=lax.Precision.HIGHEST,
    )
    raw = inner + outer_product * apply[:, None, None]
    normed = raw * lax.rsqrt(jnp.mean(raw * raw, axis=-1, keepdims=True) + 1e-06)
    mixed_lin = normed.reshape(rows, heads_here * HEAD_DIM).astype(jnp.bfloat16)
    q_heads = q_soft.reshape(shape)
    q_pos = me_index * rows + places
    scale = HEAD_DIM ** (-0.5)

    def attend(carry, piece, start):
        keys, values, ids = piece
        count = keys.shape[0] // rows
        key_blocks = keys.reshape(count, rows, heads_here, HEAD_DIM)
        value_blocks = values.reshape(count, rows, heads_here, HEAD_DIM)
        id_blocks = ids.reshape(count, rows).astype(jnp.int32)
        offsets = start + rows * jnp.arange(count, dtype=jnp.int32)

        def one_block(memory_state, block_in):
            key_block_slice, value_block_slice, id_blk, offset = block_in
            top, total, accum = memory_state
            logits = (
                jnp.einsum(
                    "thd,shd->hts", q_heads, key_block_slice, preferred_element_type=jnp.float32
                )
                * scale
            )
            key_pos = offset + places
            mask = (
                (key_pos[None, :] <= q_pos[:, None])
                & (key_pos[None, :] >= 0)
                & (id_blk[None, :] == segment[:, None])
            )
            new_top = jnp.maximum(top, jnp.max(jnp.where(mask[None], logits, -1e30), axis=-1))
            factor = jnp.exp(top - new_top)
            expo = jnp.where(mask[None], jnp.exp(logits - new_top[..., None]), 0.0)
            total = total * factor + jnp.sum(expo, axis=-1)
            added = jnp.einsum(
                "hts,shd->thd",
                expo.astype(jnp.bfloat16),
                value_block_slice,
                preferred_element_type=jnp.float32,
            )
            accum = accum * factor.T[:, :, None] + added
            memory_state = (new_top, total, accum)
            return (memory_state, None)

        carry, _ = lax.scan(one_block, carry, (key_blocks, value_blocks, id_blocks, offsets))
        return carry

    start_state = (
        jnp.full((heads_here, rows), -1e30, jnp.float32),
        jnp.zeros((heads_here, rows), jnp.float32),
        jnp.zeros(shape, jnp.float32),
    )
    ids_wire = segment.astype(jnp.bfloat16)
    seq_count = lax.axis_size("seq")
    longest = rows * seq_count * 5 // 8
    reach_steps = min(seq_count - 1, (longest - 2) // rows + 1)
    first_state = attend(start_state, (k_soft, v_soft, ids_wire), me_index * rows)

    def forward(step, loop_carry):
        memory_state, keys, values, ids = loop_carry
        keys, values, ids = shifted((keys, values, ids), "seq", 1)
        memory_state = attend(memory_state, (keys, values, ids), (me_index - step) * rows)
        return (memory_state, keys, values, ids)

    final_carry = lax.fori_loop(
        1, reach_steps + 1, forward, (first_state, k_soft, v_soft, ids_wire)
    )
    top, total, accum = final_carry[0]
    mixed_soft = (
        (accum / total.T[:, :, None]).reshape(rows, heads_here * HEAD_DIM).astype(jnp.bfloat16)
    )
    return (mixed_lin, mixed_soft)


def solution(mesh):
    in_specs = (
        P(("group", "seq"), "head"),
        P(("group", "seq"), "head"),
        P(("group", "seq"), "head"),
        P(("group", "seq"), "head"),
        P(("group", "seq"), "head"),
        P(("group", "seq"), "head"),
        P(("group", "seq")),
    )
    out_specs = (P(("group", "seq"), "head"), P(("group", "seq"), "head"))
    return jax.shard_map(
        on_device, mesh=mesh, in_specs=in_specs, out_specs=out_specs, check_vma=False
    )
```

profile of v0, /device:TPU:0, one launch (start us, length us, event | category | flops | bytes accessed | tf_op | source)
XLA Modules:
  0.0 129.4 jit_solution(17783946946622038517)
XLA Ops:
  0.6 0.0 copy-start
  0.7 0.7 fusion.56
  1.4 1.1 compare_and_fusion.1
  2.5 1.2 copy.50
  3.7 1.7 %select_reduce_fusion.1 = (f32[4,384]{1,0:T(4,128)S(1)}, f32[4,384,384]{2,1,0:T(8,128)S(1)}) fusion(pred[384,384]{1,0:T(8,128)(4,1)S(1)} %get-tuple-element.531, bf16[384,4,128]{0,2,1:T(8,128)(2,1)S(1)} %bitcast.106, bf16[384,512]{1,0:T(8,128)(2,1)} %param.15), kind=kOutput, calls=%fused_computation.24 | convolution fusion | flops 152762880 | bytes 3299328 | tf_op jit(solution)/shard_map/while/body/eval_jaxpr/thd,shd->hts/dot_general | solution.py:102
  5.5 0.9 fusion.18
  6.4 0.8 fusion.21
  7.2 0.2 copy.57
  7.4 0.2 copy.55
  7.7 0.9 copy.56
  8.6 75.5 %while.60 = (s32[]{:T(128)}, f32[4,384]{1,0:T(4,128)S(1)}, f32[4,384]{1,0:T(4,128)S(1)}, f32[384,4,128]{2,0,1:T(8,128)S(1)}, bf16[384,512]{0,1:T(8,128)(2,1)S(1)...) while((s32[]{:T(128)}, f32[4,384]{1,0:T(4,128)S(1)}, ...), condition=%wide.region_8.9_spmd.clone, body=%wide.region_5.8_spmd.clone.sunk | while | flops 309467520 | bytes 15254297 | solution.py:147
  8.6 5.1 %collective-permute-start = (bf16[384]{0:T(512)(128)(2,1)S(1)}, bf16[384]{0:T(512)(128)(2,1)S(1)}, u32[]{:S(2)}, u32[]{:S(2)}) collective-permute-start(bf16[384]{0:T(512)(128)(2,1)S(1)} %get-tuple-element.699), channel_id=1, source_target_pairs={{0,4},{4,8},{8,12},{1,5},{5,9},{9,13},{2,6},{6,10},{10,14},{3,7},{... | collective-permute-start | bytes 2312 | tf_op jit(solution)/shard_map/while/body/eval_jaxpr/ppermute | solution.py:35
  13.7 3.5 %collective-permute-start.1 = (bf16[384,512]{0,1:T(8,128)(2,1)S(1)}, bf16[384,512]{0,1:T(8,128)(2,1)S(1)}, u32[]{:S(2)}, u32[]{:S(2)}) collective-permute-start(bf16[384,512]{0,1:T(8,128)(2,1)S(1)} %get-tuple-element.697), channel_id=1, source_target_pairs={{0,4},{4,8},{8,12},{1,5},{5,9},{9,13},{2,6},{6,10},{10,14},{3,7},{... | collective-permute-start | bytes 1179656 | tf_op jit(solution)/shard_map/while/body/eval_jaxpr/ppermute | solution.py:35
  17.2 3.5 %collective-permute-start.2 = (bf16[384,512]{0,1:T(8,128)(2,1)}, bf16[384,512]{0,1:T(8,128)(2,1)S(1)}, u32[]{:S(2)}, u32[]{:S(2)}) collective-permute-start(bf16[384,512]{0,1:T(8,128)(2,1)} %get-tuple-element.698), channel_id=1, source_target_pairs={{0,4},{4,8},{8,12},{1,5},{5,9},{9,13},{2,6},{6,10},{10,14},{3,7},{... | collective-permute-start | bytes 1179656 | tf_op jit(solution)/shard_map/while/body/eval_jaxpr/ppermute | solution.py:35
  20.7 0.2 compare_and_fusion.3
  21.0 5.7 %collective-permute-done.1 = bf16[384,512]{0,1:T(8,128)(2,1)S(1)} collective-permute-done((bf16[384,512]{0,1:T(8,128)(2,1)S(1)}, bf16[384,512]{0,1:T(8,128)(2,1)S(1)}, u32[]{:S(2)}, u32[]{:S(2)}) %collective-permute-start.1) | collective-permute-done | bytes 393248 | tf_op jit(solution)/shard_map/while/body/eval_jaxpr/ppermute | solution.py:35
  26.7 0.6 select_reduce_fusion.3
  27.3 0.5 fusion.82
  27.8 5.9 %collective-permute-done.2 = bf16[384,512]{0,1:T(8,128)(2,1)S(1)} collective-permute-done((bf16[384,512]{0,1:T(8,128)(2,1)}, bf16[384,512]{0,1:T(8,128)(2,1)S(1)}, u32[]{:S(2)}, u32[]{:S(2)}) %collective-permute-start.2) | collective-permute-done | bytes 393248 | tf_op jit(solution)/shard_map/while/body/eval_jaxpr/ppermute | solution.py:35
  33.8 1.1 fusion.83
  34.9 0.7 copy.130
  35.7 4.3 %collective-permute-start = (bf16[384]{0:T(512)(128)(2,1)S(1)}, bf16[384]{0:T(512)(128)(2,1)S(1)}, u32[]{:S(2)}, u32[]{:S(2)}) collective-permute-start(bf16[384]{0:T(512)(128)(2,1)S(1)} %get-tuple-element.699), channel_id=1, source_target_pairs={{0,4},{4,8},{8,12},{1,5},{5,9},{9,13},{2,6},{6,10},{10,14},{3,7},{... | collective-permute-start | bytes 2312 | tf_op jit(solution)/shard_map/while/body/eval_jaxpr/ppermute | solution.py:35
  39.9 3.5 %collective-permute-start.1 = (bf16[384,512]{0,1:T(8,128)(2,1)S(1)}, bf16[384,512]{0,1:T(8,128)(2,1)S(1)}, u32[]{:S(2)}, u32[]{:S(2)}) collective-permute-start(bf16[384,512]{0,1:T(8,128)(2,1)S(1)} %get-tuple-element.697), channel_id=1, source_target_pairs={{0,4},{4,8},{8,12},{1,5},{5,9},{9,13},{2,6},{6,10},{10,14},{3,7},{... | collective-permute-start | bytes 1179656 | tf_op jit(solution)/shard_map/while/body/eval_jaxpr/ppermute | solution.py:35
  43.5 2.2 %collective-permute-start.2 = (bf16[384,512]{0,1:T(8,128)(2,1)}, bf16[384,512]{0,1:T(8,128)(2,1)S(1)}, u32[]{:S(2)}, u32[]{:S(2)}) collective-permute-start(bf16[384,512]{0,1:T(8,128)(2,1)} %get-tuple-element.698), channel_id=1, source_target_pairs={{0,4},{4,8},{8,12},{1,5},{5,9},{9,13},{2,6},{6,10},{10,14},{3,7},{... | collective-permute-start | bytes 1179656 | tf_op jit(solution)/shard_map/while/body/eval_jaxpr/ppermute | solution.py:35
  45.7 0.2 compare_and_fusion.3
  46.0 7.0 %collective-permute-done.1 = bf16[384,512]{0,1:T(8,128)(2,1)S(1)} collective-permute-done((bf16[384,512]{0,1:T(8,128)(2,1)S(1)}, bf16[384,512]{0,1:T(8,128)(2,1)S(1)}, u32[]{:S(2)}, u32[]{:S(2)}) %collective-permute-start.1) | collective-permute-done | bytes 393248 | tf_op jit(solution)/shard_map/while/body/eval_jaxpr/ppermute | solution.py:35
  52.9 0.6 select_reduce_fusion.3
  53.6 0.5 fusion.82
  54.1 4.8 %collective-permute-done.2 = bf16[384,512]{0,1:T(8,128)(2,1)S(1)} collective-permute-done((bf16[384,512]{0,1:T(8,128)(2,1)}, bf16[384,512]{0,1:T(8,128)(2,1)S(1)}, u32[]{:S(2)}, u32[]{:S(2)}) %collective-permute-start.2) | collective-permute-done | bytes 393248 | tf_op jit(solution)/shard_map/while/body/eval_jaxpr/ppermute | solution.py:35
  58.9 1.1 fusion.83
  60.1 0.7 copy.130
  60.8 4.3 %collective-permute-start = (bf16[384]{0:T(512)(128)(2,1)S(1)}, bf16[384]{0:T(512)(128)(2,1)S(1)}, u32[]{:S(2)}, u32[]{:S(2)}) collective-permute-start(bf16[384]{0:T(512)(128)(2,1)S(1)} %get-tuple-element.699), channel_id=1, source_target_pairs={{0,4},{4,8},{8,12},{1,5},{5,9},{9,13},{2,6},{6,10},{10,14},{3,7},{... | collective-permute-start | bytes 2312 | tf_op jit(solution)/shard_map/while/body/eval_jaxpr/ppermute | solution.py:35
  65.1 2.5 %collective-permute-start.1 = (bf16[384,512]{0,1:T(8,128)(2,1)S(1)}, bf16[384,512]{0,1:T(8,128)(2,1)S(1)}, u32[]{:S(2)}, u32[]{:S(2)}) collective-permute-start(bf16[384,512]{0,1:T(8,128)(2,1)S(1)} %get-tuple-element.697), channel_id=1, source_target_pairs={{0,4},{4,8},{8,12},{1,5},{5,9},{9,13},{2,6},{6,10},{10,14},{3,7},{... | collective-permute-start | bytes 1179656 | tf_op jit(solution)/shard_map/while/body/eval_jaxpr/ppermute | solution.py:35
  67.6 2.2 %collective-permute-start.2 = (bf16[384,512]{0,1:T(8,128)(2,1)}, bf16[384,512]{0,1:T(8,128)(2,1)S(1)}, u32[]{:S(2)}, u32[]{:S(2)}) collective-permute-start(bf16[384,512]{0,1:T(8,128)(2,1)} %get-tuple-element.698), channel_id=1, source_target_pairs={{0,4},{4,8},{8,12},{1,5},{5,9},{9,13},{2,6},{6,10},{10,14},{3,7},{... | collective-permute-start | bytes 1179656 | tf_op jit(solution)/shard_map/while/body/eval_jaxpr/ppermute | solution.py:35
  69.9 0.2 compare_and_fusion.3
  70.1 7.0 %collective-permute-done.1 = bf16[384,512]{0,1:T(8,128)(2,1)S(1)} collective-permute-done((bf16[384,512]{0,1:T(8,128)(2,1)S(1)}, bf16[384,512]{0,1:T(8,128)(2,1)S(1)}, u32[]{:S(2)}, u32[]{:S(2)}) %collective-permute-start.1) | collective-permute-done | bytes 393248 | tf_op jit(solution)/shard_map/while/body/eval_jaxpr/ppermute | solution.py:35
  77.1 0.6 select_reduce_fusion.3
  77.7 0.5 fusion.82
  78.3 4.0 %collective-permute-done.2 = bf16[384,512]{0,1:T(8,128)(2,1)S(1)} collective-permute-done((bf16[384,512]{0,1:T(8,128)(2,1)}, bf16[384,512]{0,1:T(8,128)(2,1)S(1)}, u32[]{:S(2)}, u32[]{:S(2)}) %collective-permute-start.2) | collective-permute-done | bytes 393248 | tf_op jit(solution)/shard_map/while/body/eval_jaxpr/ppermute | solution.py:35
  82.2 1.1 fusion.83
  83.4 0.7 copy.130
  84.1 1.0 copy_bitcast_fusion
  85.1 0.2 copy.66
  85.4 0.4 fusion.41
  85.8 1.6 %fusion.22 = f32[384,4,128]{0,2,1:T(8,128)S(1)} fusion(f32[4,384,384]{2,1,0:T(8,128)S(1)} %fusion.41, pred[384,384]{1,0:T(8,128)(4,1)S(1)} %get-tuple-element.532, bf16[384,512]{1,0:T(8,128)(2,1)S(1)} %copy-done.2), kind=kOutput, calls=%fused_computation.34 | convolution fusion | flops 906559488 | bytes 3686400 | tf_op jit(solution)/shard_map/hts,shd->thd/dot_general | solution.py:61
  87.5 0.6 slice.4
  88.1 0.6 compare_convert_fusion
  88.7 0.3 convolution_convert_fusion
  89.0 15.7 %all-gather = bf16[16,128,128]{2,1,0:T(8,128)(2,1)S(1)} all-gather(bf16[4,128,128]{2,1,0:T(8,128)(2,1)S(1)} %convolution_convert_fusion), channel_id=2, replica_groups=mesh['group'=2,'seq'=4,'head'=4] {'seq'}, dimensions={0}, use_global_device_ids=true | all-gather | bytes 655360 | tf_op jit(solution)/shard_map/all_gather | solution.py:12
  104.7 0.6 dynamic-slice
  106.0 0.7 dynamic-update-slice
  106.7 9.9 %all-reduce = bf16[4]{0:T(256)(128)(2,1)S(1)} all-reduce(bf16[4]{0:T(256)(128)(2,1)S(1)} %dynamic-update-slice), channel_id=1, replica_groups=mesh['group'=2,'seq'=4,'head'=4] {'seq'}, use_global_device_ids=true, to_apply=%add | all-reduce | flops 4 | bytes 16
  116.5 11.2 %while.61 = (s32[]{:T(128)}, f32[4,128,128]{2,1,0:T(8,128)S(1)}, f32[]{:T(128)}, s32[]{:T(128)}, bf16[4]{0:T(256)(128)(2,1)S(1)}, /*index=5*/bf16[4,4,128,128]{3...) while((s32[]{:T(128)}, f32[4,128,128]{2,1,0:T(8,128)S(1)}, f32[]{:T(128)}, s32[]{:T(128)}, ...), condition=%wide.region_1.2_spmd.clone, body=%wide.region_0.1_spmd.clone.sunk | while | flops 393224 | bytes 655525 | solution.py:29
  116.6 0.7 dynamic_slice.47
  118.5 0.2 select_select_fusion.2
  119.4 0.7 dynamic_slice.47
  121.3 0.2 select_select_fusion.2
  122.1 0.7 dynamic_slice.47
  124.1 0.2 select_select_fusion.2
  124.9 0.7 dynamic_slice.47
  126.9 0.2 select_select_fusion.2
  127.7 0.6 multiply_reduce_fusion
  128.4 0.1 multiply_convert_fusion
  128.5 0.9 copy.59
  (48 shorter events, 0.4 us)
Async XLA Ops:
  0.6 84.7 %copy-start = (bf16[384,512]{1,0:T(8,128)(2,1)S(1)}, bf16[384,512]{1,0:T(8,128)(2,1)}, u32[]{:S(2)}) copy-start(bf16[384,512]{1,0:T(8,128)(2,1)} %param.11) | copy-start | bytes 1179652
  3.7 2.7 %copy-start.3 = (bf16[384,512]{1,0:T(8,128)(2,1)S(1)}, bf16[384,512]{1,0:T(8,128)(2,1)}, u32[]{:S(2)}) copy-start(bf16[384,512]{1,0:T(8,128)(2,1)} %param.16) | copy-start | bytes 1179652
  6.4 1.0 copy-start.1
  7.2 1.4 %copy-start.5 = (s32[384]{0:T(512)S(1)}, s32[384]{0:T(512)}, u32[]{:S(2)}) copy-start(s32[384]{0:T(512)} %param.17) | copy-start | bytes 4612
  8.6 76.6 %copy-start.4 = (bf16[384,512]{1,0:T(8,128)(2,1)S(1)}, bf16[384,512]{1,0:T(8,128)(2,1)}, u32[]{:S(2)}) copy-start(bf16[384,512]{1,0:T(8,128)(2,1)} %param.12) | copy-start | bytes 1179652
  8.6 12.1 %collective-permute-start = (bf16[384]{0:T(512)(128)(2,1)S(1)}, bf16[384]{0:T(512)(128)(2,1)S(1)}, u32[]{:S(2)}, u32[]{:S(2)}) collective-permute-start(bf16[384]{0:T(512)(128)(2,1)S(1)} %get-tuple-element.699), channel_id=1, source_target_pairs={{0,4},{4,8},{8,12},{1,5},{5,9},{9,13},{2,6},{6,10},{10,14},{3,7},{... | collective-permute-start | bytes 2312 | tf_op jit(solution)/shard_map/while/body/eval_jaxpr/ppermute | solution.py:35
  13.7 13.0 %collective-permute-start.1 = (bf16[384,512]{0,1:T(8,128)(2,1)S(1)}, bf16[384,512]{0,1:T(8,128)(2,1)S(1)}, u32[]{:S(2)}, u32[]{:S(2)}) collective-permute-start(bf16[384,512]{0,1:T(8,128)(2,1)S(1)} %get-tuple-element.697), channel_id=1, source_target_pairs={{0,4},{4,8},{8,12},{1,5},{5,9},{9,13},{2,6},{6,10},{10,14},{3,7},{... | collective-permute-start | bytes 1179656 | tf_op jit(solution)/shard_map/while/body/eval_jaxpr/ppermute | solution.py:35
  17.2 16.6 %collective-permute-start.2 = (bf16[384,512]{0,1:T(8,128)(2,1)}, bf16[384,512]{0,1:T(8,128)(2,1)S(1)}, u32[]{:S(2)}, u32[]{:S(2)}) collective-permute-start(bf16[384,512]{0,1:T(8,128)(2,1)} %get-tuple-element.698), channel_id=1, source_target_pairs={{0,4},{4,8},{8,12},{1,5},{5,9},{9,13},{2,6},{6,10},{10,14},{3,7},{... | collective-permute-start | bytes 1179656 | tf_op jit(solution)/shard_map/while/body/eval_jaxpr/ppermute | solution.py:35
  35.7 10.0 %collective-permute-start = (bf16[384]{0:T(512)(128)(2,1)S(1)}, bf16[384]{0:T(512)(128)(2,1)S(1)}, u32[]{:S(2)}, u32[]{:S(2)}) collective-permute-start(bf16[384]{0:T(512)(128)(2,1)S(1)} %get-tuple-element.699), channel_id=1, source_target_pairs={{0,4},{4,8},{8,12},{1,5},{5,9},{9,13},{2,6},{6,10},{10,14},{3,7},{... | collective-permute-start | bytes 2312 | tf_op jit(solution)/shard_map/while/body/eval_jaxpr/ppermute | solution.py:35
  39.9 13.0 %collective-permute-start.1 = (bf16[384,512]{0,1:T(8,128)(2,1)S(1)}, bf16[384,512]{0,1:T(8,128)(2,1)S(1)}, u32[]{:S(2)}, u32[]{:S(2)}) collective-permute-start(bf16[384,512]{0,1:T(8,128)(2,1)S(1)} %get-tuple-element.697), channel_id=1, source_target_pairs={{0,4},{4,8},{8,12},{1,5},{5,9},{9,13},{2,6},{6,10},{10,14},{3,7},{... | collective-permute-start | bytes 1179656 | tf_op jit(solution)/shard_map/while/body/eval_jaxpr/ppermute | solution.py:35
  43.5 15.4 %collective-permute-start.2 = (bf16[384,512]{0,1:T(8,128)(2,1)}, bf16[384,512]{0,1:T(8,128)(2,1)S(1)}, u32[]{:S(2)}, u32[]{:S(2)}) collective-permute-start(bf16[384,512]{0,1:T(8,128)(2,1)} %get-tuple-element.698), channel_id=1, source_target_pairs={{0,4},{4,8},{8,12},{1,5},{5,9},{9,13},{2,6},{6,10},{10,14},{3,7},{... | collective-permute-start | bytes 1179656 | tf_op jit(solution)/shard_map/while/body/eval_jaxpr/ppermute | solution.py:35
  60.8 9.0 %collective-permute-start = (bf16[384]{0:T(512)(128)(2,1)S(1)}, bf16[384]{0:T(512)(128)(2,1)S(1)}, u32[]{:S(2)}, u32[]{:S(2)}) collective-permute-start(bf16[384]{0:T(512)(128)(2,1)S(1)} %get-tuple-element.699), channel_id=1, source_target_pairs={{0,4},{4,8},{8,12},{1,5},{5,9},{9,13},{2,6},{6,10},{10,14},{3,7},{... | collective-permute-start | bytes 2312 | tf_op jit(solution)/shard_map/while/body/eval_jaxpr/ppermute | solution.py:35
  65.1 12.0 %collective-permute-start.1 = (bf16[384,512]{0,1:T(8,128)(2,1)S(1)}, bf16[384,512]{0,1:T(8,128)(2,1)S(1)}, u32[]{:S(2)}, u32[]{:S(2)}) collective-permute-start(bf16[384,512]{0,1:T(8,128)(2,1)S(1)} %get-tuple-element.697), channel_id=1, source_target_pairs={{0,4},{4,8},{8,12},{1,5},{5,9},{9,13},{2,6},{6,10},{10,14},{3,7},{... | collective-permute-start | bytes 1179656 | tf_op jit(solution)/shard_map/while/body/eval_jaxpr/ppermute | solution.py:35
  67.6 14.6 %collective-permute-start.2 = (bf16[384,512]{0,1:T(8,128)(2,1)}, bf16[384,512]{0,1:T(8,128)(2,1)S(1)}, u32[]{:S(2)}, u32[]{:S(2)}) collective-permute-start(bf16[384,512]{0,1:T(8,128)(2,1)} %get-tuple-element.698), channel_id=1, source_target_pairs={{0,4},{4,8},{8,12},{1,5},{5,9},{9,13},{2,6},{6,10},{10,14},{3,7},{... | collective-permute-start | bytes 1179656 | tf_op jit(solution)/shard_map/while/body/eval_jaxpr/ppermute | solution.py:35
  84.1 1.7 %copy-start.2 = (bf16[384,512]{1,0:T(8,128)(2,1)S(1)}, bf16[384,512]{1,0:T(8,128)(2,1)}, u32[]{:S(2)}) copy-start(bf16[384,512]{1,0:T(8,128)(2,1)} %param.13) | copy-start | bytes 1179652
  85.8 18.9 %copy-start.6 = (u32[32]{0:T(128)S(1)}, u32[32]{0:T(128)}, u32[]{:S(2)}) copy-start(u32[32]{0:T(128)} %constant.136) | copy-start | bytes 388
where the time goes:
time: 130 us; the launch traced here: 129 us
  waiting for transfers between devices  34.3 us (26%)
  starting transfers between devices  31 us (24%)
  blocking collectives  25.6 us (20%)
  local copies, waits for them, and re-layouts  10.7 us (8%)
  matrix products  10.6 us (8%)
  loops' own time  8.13 us (6%)
  other arithmetic  7.61 us (6%)
  between operations  1.49 us (1%)
    ppermute x9, waiting for transfers between devices, shifted(): lax.ppermute(value, axis, [(source, source + steps) for source in range(i...  34.3 us
    ppermute x9, starting transfers between devices, shifted(): lax.ppermute(value, axis, [(source, source + steps) for source in range(i...  31 us
    all_gather x1, blocking collectives, entering(): lax.all_gather(part.astype(kind), axis)  15.7 us
    unnamed x1, blocking collectives  9.86 us
    another operation x1, loops' own time, entering(): return lax.fori_loop(0, devices, hop, start)  7.79 us
    unnamed x22, local copies, waits for them, and re-layouts  4.88 us
    dot_general x4, matrix products, one_block(): jnp.einsum('hts,shd->thd', expo.astype(jnp.bfloat16), value_block_slice,...  4.03 us
    dot_general x4, matrix products, one_block(): jnp.einsum('thd,shd->hts', q_heads, key_block_slice, preferred_element_ty...  3.59 us
  transfers between devices with their start and end apart: 9, of which 6 were waited for; matrix products, arithmetic and copies ran while one was open for 3% of the time, Pallas kernels for 0%

commit v1 on v0

--- a/solution.py
+++ b/solution.py
@@ -1,6 +1,11 @@
+import functools
+import math
+
 import jax
 import jax.numpy as jnp
 from jax import lax
+from jax.experimental import pallas as pl
+from jax.experimental.pallas import tpu as pltpu
 from jax.sharding import PartitionSpec as P
 
 HEAD_DIM = 128
@@ -154,6 +159,344 @@
     return (mixed_lin, mixed_soft)
 
 
+D = HEAD_DIM
+BF, F32 = jnp.bfloat16, jnp.float32
+OTHER = -65536.0
+HIDDEN = -1e30
+SCALE2 = D ** (-0.5) * math.log2(math.e)
+K_IN, V_IN, Q_A, Q_B, O_A, M_A, O_B, M_B, STATE = range(9)
+KINDS = 9
+
+
+def nt(a, b):
+    return lax.dot_general(a, b, (((1,), (1,)), ((), ())), preferred_element_type=F32)
+
+
+def tn(a, b):
+    return lax.dot_general(a, b, (((0,), (0,)), ((), ())), preferred_element_type=F32)
+
+
+def softmax_part(pieces, query):
+    scores = []
+    for keys, _, bias in pieces:
+        s = nt(keys, query)
+        scores.append(s if bias is None else s + bias)
+    top = functools.reduce(jnp.maximum, [jnp.max(s, axis=0, keepdims=True) for s in scores])
+    total, out = 0.0, 0.0
+    for s, (_, values, _) in zip(scores, pieces):
+        p = jnp.exp2((s - top) * SCALE2)
+        total = total + jnp.sum(p, axis=0, keepdims=True)
+        out = out + tn(values, p.astype(BF))
+    return top * SCALE2, total, out
+
+
+def kernel(
+    rows, heads, low,
+    ql_h, kl_h, vl_h, qs_h, ks_h, vs_h, seg,
+    out_l, out_s,
+    ql, kl, vl, qs, ks, vs,
+    k_in, v_in, q_a, q_b, segs, o_a, m_a, o_b, m_b, state_in,
+    o_to_a, m_to_a, o_to_b, m_to_b, state_out,
+    bias, e_own, f_own, own_o, own_m, own_l,
+    local_sem, seg_send, seg_recv, send_sem, recv_sem,
+):
+    me = lax.axis_index("seq")
+    n = 4
+    arrays = ((ql_h, ql), (kl_h, kl), (vl_h, vl), (qs_h, qs), (ks_h, ks), (vs_h, vs))
+    loads = [
+        pltpu.make_async_copy(a, b, local_sem.at[i]) for i, (a, b) in enumerate(arrays)
+    ]
+    for load in loads:
+        load.start()
+
+    barrier = pltpu.get_barrier_semaphore()
+    for step in range(1, n):
+        pl.semaphore_signal(
+            barrier, inc=1, device_id={"seq": lax.rem(me + step, n)},
+            device_id_type=pl.DeviceIdType.MESH,
+        )
+    pl.semaphore_wait(barrier, n - 1)
+
+    def copy(kind, h, src, dst, to):
+        return pltpu.make_async_remote_copy(
+            src_ref=src, dst_ref=dst,
+            send_sem=send_sem.at[kind, h], recv_sem=recv_sem.at[kind, h],
+            device_id={"seq": to}, device_id_type=pl.DeviceIdType.MESH,
+        )
+
+    def seg_copy(owner, to):
+        return pltpu.make_async_remote_copy(
+            src_ref=seg, dst_ref=segs.at[owner],
+            send_sem=seg_send.at[to], recv_sem=seg_recv.at[owner],
+            device_id={"seq": to}, device_id_type=pl.DeviceIdType.MESH,
+        )
+
+    def cols(h):
+        return pl.ds(pl.multiple_of(h * D, D), D)
+
+    def each_head(body):
+        def run(h, carry):
+            body(h)
+            return carry
+        lax.fori_loop(0, heads, run, 0)
+
+    def column(row):
+        return jnp.broadcast_to(row.astype(F32), (D, rows)).T
+
+    lane = lax.broadcasted_iota(jnp.int32, (rows, D), 1).astype(F32)
+
+    def query_side(row):
+        return jnp.where(column(row) == lane, 1.0, 0.0).astype(BF)
+
+    def key_side(row):
+        return jnp.where(column(row) == lane, 0.0, OTHER).astype(BF)
+
+    def put(ref, h, value):
+        ref[:, cols(h)] = value.T.astype(BF)
+
+    def prepare():
+        row = seg[...]
+        frow = row.astype(F32)
+        square = jnp.broadcast_to(frow, (rows, rows))
+        s = lax.broadcasted_iota(jnp.int32, (rows, rows), 0)
+        t = lax.broadcasted_iota(jnp.int32, (rows, rows), 1)
+        bias[...] = jnp.where((s <= t) & (square.T == square), 0.0, HIDDEN)
+        e_own[...] = query_side(row)
+        f_own[...] = key_side(row)
+
+    def own_keys(h):
+        return jnp.concatenate([ks[:, cols(h)], f_own[...]], axis=1)
+
+    def own_query(h):
+        return jnp.concatenate([qs[:, cols(h)], e_own[...]], axis=1)
+
+    def linear(h, d):
+        k, v, q = kl[:, cols(h)], vl[:, cols(h)], ql[:, cols(h)]
+        frow = seg[...].astype(F32)
+        if d > 0:
+            before = segs[d - 1].astype(F32)[:, rows - 1:]
+            copy(STATE, h, state_out.at[h], state_in.at[h], d).wait_recv()
+            arrived = state_in[h]
+        if d < n - 1:
+            kept = (column(seg[...]) == frow[:, rows - 1:]).astype(F32)
+            state = tn((v.astype(F32) * kept).astype(BF), k)
+            if d > 0:
+                state = state + jnp.where(before == frow[:, rows - 1:], arrived.astype(F32), 0.0)
+            state_out[h] = state.astype(BF)
+            copy(STATE, h, state_out.at[h], state_in.at[h], d + 1).start()
+        a = jnp.where(bias[...] == 0.0, nt(k, q), 0.0)
+        raw = tn(v, a.astype(BF))
+        if d > 0:
+            raw = raw + jnp.where(frow == before, nt(arrived, q), 0.0)
+        mean = jnp.mean(raw * raw, axis=0, keepdims=True)
+        put(out_l, h, raw * lax.rsqrt(mean + 1e-06))
+
+    def keep_own(h):
+        m, l, o = softmax_part([(own_keys(h), vs[:, cols(h)], bias[...])], own_query(h))
+        own_o[h] = o
+        own_m[h] = jnp.broadcast_to(m, (8, rows))
+        own_l[h] = jnp.broadcast_to(l, (8, rows))
+
+    def merge(h, others):
+        m, l, o = own_m[h][:1], own_l[h][:1], own_o[h]
+        sides = [(r_m[h][:1], r_o[h].astype(F32)) for r_o, r_m in others]
+        top = functools.reduce(jnp.maximum, [x for x, _ in sides], m)
+        w = jnp.exp2(m - top)
+        total, out = l * w, o * w
+        for x, y in sides:
+            w = jnp.exp2(x - top)
+            total, out = total + w, out + y * w
+        put(out_s, h, out / total)
+
+    def send_part(h, pieces, query, o_ref, m_ref, o_dst, m_dst, o_kind, m_kind, to):
+        m, l, o = softmax_part(pieces, query)
+        o_ref[h] = (o / l).astype(BF)
+        m_ref[h] = jnp.broadcast_to(m + jnp.log(l) * math.log2(math.e), (8, rows))
+        copy(o_kind, h, o_ref.at[h], o_dst.at[h], to).start()
+        copy(m_kind, h, m_ref.at[h], m_dst.at[h], to).start()
+
+    def load_all():
+        for load in loads:
+            load.wait()
+
+    @pl.when(me == 0)
+    def _():
+        seg_copy(0, 1).start()
+        for h in range(heads):
+            c = slice(h * D, (h + 1) * D)
+            copy(K_IN, h, ks_h.at[:, c], k_in.at[:, c], 1).start()
+            copy(V_IN, h, vs_h.at[:, c], v_in.at[:, c], 1).start()
+        prepare()
+        load_all()
+
+        def first(h):
+            linear(h, 0)
+            m, l, o = softmax_part([(own_keys(h), vs[:, cols(h)], bias[...])], own_query(h))
+            put(out_s, h, o / l)
+
+        each_head(first)
+        seg_copy(0, 1).wait_send()
+        for h in range(heads):
+            c = slice(h * D, (h + 1) * D)
+            copy(K_IN, h, ks_h.at[:, c], k_in.at[:, c], 1).wait_send()
+            copy(V_IN, h, vs_h.at[:, c], v_in.at[:, c], 1).wait_send()
+            copy(STATE, h, state_out.at[h], state_in.at[h], 1).wait_send()
+
+    @pl.when(me == 1)
+    def _():
+        seg_copy(1, 2).start()
+        prepare()
+        load_all()
+        seg_copy(0, 1).wait_recv()
+        each_head(lambda h: linear(h, 1))
+        for owner in (2, 3):
+            seg_copy(owner, 1).wait_recv()
+        f_0 = key_side(segs[0])
+        e_a, e_b = query_side(segs[2]), query_side(segs[3])
+
+        def middle(h):
+            c = cols(h)
+            copy(K_IN, h, ks_h.at[:, c], k_in.at[:, c], 1).wait_recv()
+            copy(V_IN, h, vs_h.at[:, c], v_in.at[:, c], 1).wait_recv()
+            copy(Q_A, h, qs_h.at[:, c], q_a.at[:, c], 1).wait_recv()
+            keys = jnp.concatenate([k_in[:, c], f_0], axis=1)
+            values = v_in[:, c]
+            own = (own_keys(h), vs[:, c], None)
+            send_part(
+                h, [(keys, values, None), own], jnp.concatenate([q_a[:, c], e_a], axis=1),
+                o_to_a, m_to_a, o_a, m_a, O_A, M_A, 2,
+            )
+            m, l, o = softmax_part(
+                [(keys, values, None), (own_keys(h), vs[:, c], bias[...])], own_query(h)
+            )
+            put(out_s, h, o / l)
+            copy(Q_B, h, qs_h.at[:, c], q_b.at[:, c], 1).wait_recv()
+            send_part(
+                h, [(keys[low:], values[low:], None), own],
+                jnp.concatenate([q_b[:, c], e_b], axis=1),
+                o_to_b, m_to_b, o_b, m_b, O_B, M_B, 3,
+            )
+
+        each_head(middle)
+        seg_copy(1, 2).wait_send()
+        for h in range(heads):
+            copy(STATE, h, state_out.at[h], state_in.at[h], 2).wait_send()
+            copy(O_A, h, o_to_a.at[h], o_a.at[h], 2).wait_send()
+            copy(M_A, h, m_to_a.at[h], m_a.at[h], 2).wait_send()
+            copy(O_B, h, o_to_b.at[h], o_b.at[h], 3).wait_send()
+            copy(M_B, h, m_to_b.at[h], m_b.at[h], 3).wait_send()
+
+    @pl.when(me == 2)
+    def _():
+        seg_copy(2, 1).start()
+        seg_copy(2, 3).start()
+        for h in range(heads):
+            c = slice(h * D, (h + 1) * D)
+            copy(Q_A, h, qs_h.at[:, c], q_a.at[:, c], 1).start()
+        prepare()
+        load_all()
+        seg_copy(3, 2).wait_recv()
+        e_a = query_side(segs[3])
+
+        def last(h):
+            c = cols(h)
+            copy(Q_A, h, qs_h.at[:, c], q_a.at[:, c], 2).wait_recv()
+            send_part(
+                h, [(own_keys(h), vs[:, c], None)], jnp.concatenate([q_a[:, c], e_a], axis=1),
+                o_to_a, m_to_a, o_a, m_a, O_A, M_A, 3,
+            )
+
+        each_head(last)
+        seg_copy(1, 2).wait_recv()
+        each_head(lambda h: linear(h, 2))
+        each_head(keep_own)
+
+        def finish(h):
+            copy(O_A, h, o_to_a.at[h], o_a.at[h], 2).wait_recv()
+            copy(M_A, h, m_to_a.at[h], m_a.at[h], 2).wait_recv()
+            merge(h, [(o_a, m_a)])
+
+        each_head(finish)
+        seg_copy(2, 1).wait_send()
+        seg_copy(2, 3).wait_send()
+        for h in range(heads):
+            c = slice(h * D, (h + 1) * D)
+            copy(Q_A, h, qs_h.at[:, c], q_a.at[:, c], 1).wait_send()
+            copy(STATE, h, state_out.at[h], state_in.at[h], 3).wait_send()
+            copy(O_A, h, o_to_a.at[h], o_a.at[h], 3).wait_send()
+            copy(M_A, h, m_to_a.at[h], m_a.at[h], 3).wait_send()
+
+    @pl.when(me == 3)
+    def _():
+        seg_copy(3, 2).start()
+        seg_copy(3, 1).start()
+        for kind, dst, to in ((Q_A, q_a, 2), (Q_B, q_b, 1)):
+            for h in range(heads):
+                c = slice(h * D, (h + 1) * D)
+                copy(kind, h, qs_h.at[:, c], dst.at[:, c], to).start()
+        prepare()
+        load_all()
+        each_head(keep_own)
+        seg_copy(2, 3).wait_recv()
+        each_head(lambda h: linear(h, 3))
+
+        def finish(h):
+            copy(O_A, h, o_to_a.at[h], o_a.at[h], 3).wait_recv()
+            copy(M_A, h, m_to_a.at[h], m_a.at[h], 3).wait_recv()
+            copy(O_B, h, o_to_b.at[h], o_b.at[h], 3).wait_recv()
+            copy(M_B, h, m_to_b.at[h], m_b.at[h], 3).wait_recv()
+            merge(h, [(o_a, m_a), (o_b, m_b)])
+
+        each_head(finish)
+        seg_copy(3, 2).wait_send()
+        seg_copy(3, 1).wait_send()
+        for kind, dst, to in ((Q_A, q_a, 2), (Q_B, q_b, 1)):
+            for h in range(heads):
+                c = slice(h * D, (h + 1) * D)
+                copy(kind, h, qs_h.at[:, c], dst.at[:, c], to).wait_send()
+
+
+def four_devices(q_lin, k_lin, v_lin, q_soft, k_soft, v_soft, segment):
+    rows, width = q_lin.shape
+    heads = width // D
+    longest = rows * 4 * 5 // 8
+    low = max(0, (3 * rows - longest + 1) // 16 * 16)
+    block = pltpu.VMEM((rows, width), BF)
+    part = pltpu.VMEM((heads, D, rows), BF)
+    stat = pltpu.VMEM((heads, 8, rows), F32)
+    state = pltpu.VMEM((heads, D, D), BF)
+    out = jax.ShapeDtypeStruct((rows, width), BF)
+    vmem = pl.BlockSpec(memory_space=pltpu.VMEM)
+    return pl.pallas_call(
+        functools.partial(kernel, rows, heads, low),
+        out_shape=(out, out),
+        in_specs=[pl.BlockSpec(memory_space=pl.ANY)] * 6 + [vmem],
+        out_specs=(vmem, vmem),
+        scratch_shapes=[block] * 6
+        + [block] * 4
+        + [pltpu.VMEM((4, 1, rows), jnp.int32), part, stat, part, stat, state]
+        + [part, stat, part, stat, state]
+        + [
+            pltpu.VMEM((rows, rows), F32),
+            pltpu.VMEM((rows, D), BF),
+            pltpu.VMEM((rows, D), BF),
+            pltpu.VMEM((heads, D, rows), F32),
+            stat,
+            stat,
+        ]
+        + [
+            pltpu.SemaphoreType.DMA((6,)),
+            pltpu.SemaphoreType.DMA((4,)),
+            pltpu.SemaphoreType.DMA((4,)),
+            pltpu.SemaphoreType.DMA((KINDS, heads)),
+            pltpu.SemaphoreType.DMA((KINDS, heads)),
+        ],
+        compiler_params=pltpu.CompilerParams(
+            collective_id=0, has_side_effects=True, vmem_limit_bytes=48 * 1024 * 1024
+        ),
+    )(q_lin, k_lin, v_lin, q_soft, k_soft, v_soft, segment.reshape(1, rows))
+
+
 def solution(mesh):
     in_specs = (
         P(("group", "seq"), "head"),
@@ -166,5 +509,5 @@
     )
     out_specs = (P(("group", "seq"), "head"), P(("group", "seq"), "head"))
     return jax.shard_map(
-        on_device, mesh=mesh, in_specs=in_specs, out_specs=out_specs, check_vma=False
-    )
+        four_devices if mesh.shape["seq"] == 4 else on_device, mesh=mesh, in_specs=in_specs, out_specs=out_specs, check_vma=False
+    )

time: 130 us -> 57.4 us (0.44)
  the two profiles are of different devices: /device:TPU:0 before, /device:TPU:30 now
where the time goes in v1:
time: 57.4 us; the launch traced here: 57 us
  Pallas kernels  48.2 us (84%)
  local copies, waits for them, and re-layouts  8.15 us (14%)
  between operations  0.64 us (1%)
    pallas_call x1, Pallas kernels, four_devices(): pl.pallas_call(functools.partial(kernel, rows, heads, low), out_shape=(ou...  48.2 us
    unnamed x14, local copies, waits for them, and re-layouts  7.47 us

profile of v1, /device:TPU:30, one launch (start us, length us, event | category | flops | bytes accessed | tf_op | source)
XLA Modules:
  0.0 57.0 jit_solution(4546089020742282279)
XLA Ops:
  0.6 0.7 %reshape.7.seg = s32[1,384]{1,0:T(1,128)S(1)} reshape(s32[384]{0:T(512)} %param.13) | data formatting | bytes 3072 | tf_op jit(solution)/shard_map/reshape | solution.py:497
  1.3 0.0 copy-start
  1.3 1.0 %copy-done = bf16[384,512]{1,0:T(8,128)(2,1)S(1)} copy-done((bf16[384,512]{1,0:T(8,128)(2,1)S(1)}, bf16[384,512]{1,0:T(8,128)(2,1)}, u32[]{:S(2)}) %copy-start) | copy-done | bytes 393240
  2.3 0.0 copy-start.1
  2.3 1.0 %copy-done.1 = bf16[384,512]{1,0:T(8,128)(2,1)S(1)} copy-done((bf16[384,512]{1,0:T(8,128)(2,1)S(1)}, bf16[384,512]{1,0:T(8,128)(2,1)}, u32[]{:S(2)}) %copy-start.1) | copy-done | bytes 393240
  3.3 0.0 copy-start.2
  3.3 1.0 %copy-done.2 = bf16[384,512]{1,0:T(8,128)(2,1)S(1)} copy-done((bf16[384,512]{1,0:T(8,128)(2,1)S(1)}, bf16[384,512]{1,0:T(8,128)(2,1)}, u32[]{:S(2)}) %copy-start.2) | copy-done | bytes 393240
  4.3 0.0 copy-start.3
  4.3 1.0 %copy-done.3 = bf16[384,512]{1,0:T(8,128)(2,1)S(1)} copy-done((bf16[384,512]{1,0:T(8,128)(2,1)S(1)}, bf16[384,512]{1,0:T(8,128)(2,1)}, u32[]{:S(2)}) %copy-start.3) | copy-done | bytes 393240
  5.3 0.0 copy-start.4
  5.3 1.0 %copy-done.4 = bf16[384,512]{1,0:T(8,128)(2,1)S(1)} copy-done((bf16[384,512]{1,0:T(8,128)(2,1)S(1)}, bf16[384,512]{1,0:T(8,128)(2,1)}, u32[]{:S(2)}) %copy-start.4) | copy-done | bytes 393240
  6.3 0.0 copy-start.5
  6.3 1.0 %copy-done.5 = bf16[384,512]{1,0:T(8,128)(2,1)S(1)} copy-done((bf16[384,512]{1,0:T(8,128)(2,1)S(1)}, bf16[384,512]{1,0:T(8,128)(2,1)}, u32[]{:S(2)}) %copy-start.5) | copy-done | bytes 393240
  7.3 48.2 %shard_map.86 = (bf16[384,512]{1,0:T(8,128)(2,1)S(1)}, bf16[384,512]{1,0:T(8,128)(2,1)S(1)}) custom-call(bf16[384,512]{1,0:T(8,128)(2,1)S(1)} %copy-done, bf16[384,512]{1,0:T(8,128)(2,1)S(1)} %copy-done.1, bf16[384,512]{1,0:T(8,128)(2,1)S(1)} %copy-done.2, bf16[384,512]{1,0:T(8,128)(2,1)S(1)} %copy-done.3, bf16[384,512]{1,0:T(8,128)(2,1)S(1)} %copy-done.4, ...), custom_call_target="tpu_custom_call" | custom-call | tf_op jit(solution)/shard_map/pallas_call | solution.py:470
  55.5 0.7 %copy.11 = bf16[384,512]{1,0:T(8,128)(2,1)} copy(bf16[384,512]{1,0:T(8,128)(2,1)S(1)} %get-tuple-element.4) | data formatting | bytes 786432
  56.3 0.7 %copy.12 = bf16[384,512]{1,0:T(8,128)(2,1)} copy(bf16[384,512]{1,0:T(8,128)(2,1)S(1)} %get-tuple-element.5) | data formatting | bytes 786432
Async XLA Ops:
  1.3 1.0 %copy-start = (bf16[384,512]{1,0:T(8,128)(2,1)S(1)}, bf16[384,512]{1,0:T(8,128)(2,1)}, u32[]{:S(2)}) copy-start(bf16[384,512]{1,0:T(8,128)(2,1)} %ql_h.1) | copy-start | bytes 1179652
  2.3 1.0 %copy-start.1 = (bf16[384,512]{1,0:T(8,128)(2,1)S(1)}, bf16[384,512]{1,0:T(8,128)(2,1)}, u32[]{:S(2)}) copy-start(bf16[384,512]{1,0:T(8,128)(2,1)} %kl_h.1) | copy-start | bytes 1179652
  3.3 1.0 %copy-start.2 = (bf16[384,512]{1,0:T(8,128)(2,1)S(1)}, bf16[384,512]{1,0:T(8,128)(2,1)}, u32[]{:S(2)}) copy-start(bf16[384,512]{1,0:T(8,128)(2,1)} %vl_h.1) | copy-start | bytes 1179652
  4.3 1.0 %copy-start.3 = (bf16[384,512]{1,0:T(8,128)(2,1)S(1)}, bf16[384,512]{1,0:T(8,128)(2,1)}, u32[]{:S(2)}) copy-start(bf16[384,512]{1,0:T(8,128)(2,1)} %qs_h.1) | copy-start | bytes 1179652
  5.3 1.0 %copy-start.4 = (bf16[384,512]{1,0:T(8,128)(2,1)S(1)}, bf16[384,512]{1,0:T(8,128)(2,1)}, u32[]{:S(2)}) copy-start(bf16[384,512]{1,0:T(8,128)(2,1)} %ks_h.1) | copy-start | bytes 1179652
  6.3 1.0 %copy-start.5 = (bf16[384,512]{1,0:T(8,128)(2,1)S(1)}, bf16[384,512]{1,0:T(8,128)(2,1)}, u32[]{:S(2)}) copy-start(bf16[384,512]{1,0:T(8,128)(2,1)} %vs_h.1) | copy-start | bytes 1179652
